TPU v7x, 32 devices: a whole 2x2x4 slice. The times are simulated.
32 devices in a mesh: dp: 2 (over x), ctx: 4 (over z), tp: 4 (over y, core).
Axes of the slice: x: 2, y: 2, z: 4, core: 2. Of those that a mesh axis runs over, the one named last changes fastest.
Arguments:
- hidden_in: bfloat16 [2, 2, 2048, 768], P(None, 'dp', 'ctx'), may hold values from -6 to 6
- prefix: int32 [2, 2], P(None, 'dp'), may hold values from 204 to 1024
- block_order: int32 [8], replicated, may hold values from 0 to 7, each once
- qkv_weight: bfloat16 [3, 768, 768], P(None, 'dp', 'tp'), may hold values from -0.3125 to 0.3125
- out_weight: bfloat16 [768, 768], P('tp', 'dp'), may hold values from -2.5 to 2.5
- up_weight: bfloat16 [768, 3072], P('dp', 'tp'), may hold values from -0.21875 to 0.21875
- down_weight: bfloat16 [3072, 768], P('tp', 'dp'), may hold values from -0.4375 to 0.4375
- ln_gains: bfloat16 [2, 768], P(None, 'dp'), may hold values from 0.5 to 1.5
- ln_shifts: bfloat16 [2, 768], P(None, 'dp'), may hold values from -2 to 2
- cotangent: bfloat16 [2, 2, 2048, 768], P(None, 'dp', 'ctx'), may hold values from -6 to 6
Outputs:
- block_out: bfloat16 [2, 2, 2048, 768], P(None, 'dp', 'ctx')
- grad_in: float32 [2, 2, 2048, 768], P(None, 'dp', 'ctx')
- grad_qkv: float32 [3, 768, 768], P(None, 'dp', 'tp')
- grad_out: float32 [768, 768], P('tp', 'dp')
- grad_up: float32 [768, 3072], P('dp', 'tp')
- grad_down: float32 [3072, 768], P('tp', 'dp')
- grad_gains: float32 [2, 768], P(None, 'dp')
- grad_shifts: float32 [2, 768], P(None, 'dp')
Inputs may be any that keep to these rules, and one draw needn't show every extreme that they name: `prefix`: leading positions of each sequence that all of its queries see. `block_order`: each of the 2 * 4 block numbers appears once.
All inputs are finite; a program needn't handle non-finite values.
Results may differ from a plain program's by a relative error of at most 0.012.
The roundings to bfloat16 on the way count: a program that leaves them out, or rounds other values in their place, can miss the bound.
Values may be sent and summed in bfloat16 or wider, within the bound.
A program may use at most 128 MiB of HBM per device.

v0:
```python
import jax
import jax.numpy as jnp
from jax import lax
from jax.sharding import PartitionSpec as P

HEAD_DIM = 64
DEPTH = 12
EPS = 1e-05
GELU_C = 0.7978845608028654
GELU_A = 0.044715
NEG = -1e30
ROW_BLOCK = 512


def apply_layer_norm(values, norm_gain, norm_shift):
    row_mean = jnp.mean(values, axis=1, keepdims=True)
    centered_input = values - row_mean
    inverse_deviation = lax.rsqrt(
        jnp.mean(centered_input * centered_input, axis=1, keepdims=True) + EPS
    )
    normalized_input = centered_input * inverse_deviation
    return (normalized_input * norm_gain + norm_shift, normalized_input, inverse_deviation)


def norm_backward(normed_gradient, normalized_input, inverse_deviation, norm_gain):
    scaled_gradient = normed_gradient * norm_gain
    return inverse_deviation * (
        scaled_gradient
        - jnp.mean(scaled_gradient, axis=1, keepdims=True)
        - normalized_input * jnp.mean(scaled_gradient * normalized_input, axis=1, keepdims=True)
    )


def gelu_value(u):
    return 0.5 * u * (1.0 + jnp.tanh(GELU_C * (u + GELU_A * u * u * u)))


def gelu_slope(u):
    inner = jnp.tanh(GELU_C * (u + GELU_A * u * u * u))
    return 0.5 * (1.0 + inner) + 0.5 * u * (1.0 - inner * inner) * GELU_C * (
        1.0 + 3.0 * GELU_A * u * u
    )


def block_positions(block_order, rows, half):
    slots = jnp.arange(block_order.shape[0], dtype=jnp.int32)
    picked = jnp.where((rows // half)[:, None] == slots[None, :], block_order[None, :], 0)
    return jnp.sum(picked, axis=1) * half + rows % half


def fetch_weights(qkv_weight, out_weight, up_weight, down_weight, ln_gains, ln_shifts):
    return (
        lax.all_gather(qkv_weight, "dp", axis=1, tiled=True),
        lax.all_gather(out_weight, "dp", axis=1, tiled=True),
        lax.all_gather(up_weight, "dp", axis=0, tiled=True),
        lax.all_gather(down_weight, "dp", axis=1, tiled=True),
        lax.all_gather(ln_gains, "dp", axis=1, tiled=True),
        lax.all_gather(ln_shifts, "dp", axis=1, tiled=True),
    )


def body(
    hidden_in,
    prefix,
    block_order,
    qkv_weight,
    out_weight,
    up_weight,
    down_weight,
    ln_gains,
    ln_shifts,
    cotangent,
):
    micro = hidden_in.shape[0]
    tokens = hidden_in.shape[2]
    width = hidden_in.shape[3]
    local_width = qkv_weight.shape[2]
    head_dim = HEAD_DIM
    local_heads = local_width // head_dim
    seq_len = tokens * lax.axis_size("ctx")
    half = tokens // 2
    branch = DEPTH ** (-0.5)
    scale = head_dim ** (-0.5)
    block_rows = min(tokens, ROW_BLOCK)
    blocks = tokens // block_rows
    query_rows = lax.axis_index("ctx") * tokens + jnp.arange(tokens, dtype=jnp.int32)
    key_rows = jnp.arange(seq_len, dtype=jnp.int32)
    query_pos = block_positions(block_order, query_rows, half)
    key_pos = block_positions(block_order, key_rows, half)
    acc_qkv = jnp.zeros((3, width, local_width), jnp.float32)
    acc_out = jnp.zeros((local_width, width), jnp.float32)
    acc_up = jnp.zeros((width, up_weight.shape[1]), jnp.float32)
    acc_down = jnp.zeros((down_weight.shape[0], width), jnp.float32)
    acc_gains = jnp.zeros((2, width), jnp.float32)
    acc_shifts = jnp.zeros((2, width), jnp.float32)
    results = []
    input_gradient_list = []
    for index in range(micro):
        full = fetch_weights(qkv_weight, out_weight, up_weight, down_weight, ln_gains, ln_shifts)
        qkv_full, out_full, up_full, down_full, gains_full, shifts_full = full
        norm_gains = gains_full.astype(jnp.float32)
        norm_shifts = shifts_full.astype(jnp.float32)
        input_rows = hidden_in[index, 0].astype(jnp.float32)
        allowed = (key_pos[None, :] <= query_pos[:, None]) | (key_pos[None, :] < prefix[index, 0])
        first_normed, normalized_first1, inverse_deviation1 = apply_layer_norm(
            input_rows, norm_gains[0], norm_shifts[0]
        )
        h1 = first_normed.astype(jnp.bfloat16)
        qkv = jnp.einsum("td,kde->kte", h1, qkv_full, preferred_element_type=jnp.float32).astype(
            jnp.bfloat16
        )
        keys_flat, values_flat = (
            lax.all_gather(qkv[1], "ctx", axis=0, tiled=True),
            lax.all_gather(qkv[2], "ctx", axis=0, tiled=True),
        )
        keys = keys_flat.reshape(seq_len, local_heads, head_dim)
        values = values_flat.reshape(seq_len, local_heads, head_dim)
        q_blocks = qkv[0].reshape(blocks, block_rows, local_heads, head_dim)
        a_blocks = allowed.reshape(blocks, block_rows, seq_len)

        def attend(item):
            q_blk, allow_blk = item
            scores = (
                jnp.einsum("qhd,khd->hqk", q_blk, keys, preferred_element_type=jnp.float32) * scale
            )
            scores = jnp.where(allow_blk[None], scores, NEG)
            top = jnp.max(scores, axis=2, keepdims=True)
            expd = jnp.exp(scores - top)
            total = jnp.sum(expd, axis=2, keepdims=True)
            prob = (expd / total).astype(jnp.bfloat16)
            mixed = jnp.einsum("hqk,khd->qhd", prob, values, preferred_element_type=jnp.float32)
            return (mixed.astype(jnp.bfloat16), (top + jnp.log(total))[:, :, 0])

        heads_out, logsum = lax.map(attend, (q_blocks, a_blocks))
        heads = heads_out.reshape(tokens, local_width)
        attn_part = jnp.dot(heads, out_full, preferred_element_type=jnp.float32)
        attn = lax.psum(attn_part, "tp")
        middle_state = input_rows + branch * attn
        second_normed, normalized_second2, inverse_deviation2 = apply_layer_norm(
            middle_state, norm_gains[1], norm_shifts[1]
        )
        h2 = second_normed.astype(jnp.bfloat16)
        up = jnp.dot(h2, up_full, preferred_element_type=jnp.float32)
        act = gelu_value(up).astype(jnp.bfloat16)
        mlp_part = jnp.dot(act, down_full, preferred_element_type=jnp.float32)
        mlp = lax.psum(mlp_part, "tp")
        results.append((middle_state + branch * mlp).astype(jnp.bfloat16))
        qkv_full, out_full, up_full, down_full, gains_full, shifts_full = fetch_weights(
            qkv_weight, out_weight, up_weight, down_weight, ln_gains, ln_shifts
        )
        upstream_gradient = cotangent[index, 0].astype(jnp.float32)
        d_mlp = (branch * upstream_gradient).astype(jnp.bfloat16)
        grad_down = jnp.einsum("tf,td->fd", act, d_mlp, preferred_element_type=jnp.float32)
        d_act = jnp.einsum("td,fd->tf", d_mlp, down_full, preferred_element_type=jnp.float32)
        d_up = (d_act * gelu_slope(up)).astype(jnp.bfloat16)
        grad_up = jnp.einsum("td,tf->df", h2, d_up, preferred_element_type=jnp.float32)
        n2_back = jnp.einsum("tf,df->td", d_up, up_full, preferred_element_type=jnp.float32)
        second_norm_gradient = lax.psum(n2_back, "tp")
        middle_gradient = upstream_gradient + norm_backward(
            second_norm_gradient, normalized_second2, inverse_deviation2, norm_gains[1]
        )
        d_attn = (branch * middle_gradient).astype(jnp.bfloat16)
        grad_out = jnp.einsum("te,td->ed", heads, d_attn, preferred_element_type=jnp.float32)
        d_heads = jnp.einsum(
            "td,ed->te", d_attn, out_full, preferred_element_type=jnp.float32
        ).astype(jnp.bfloat16)
        dh_blocks = d_heads.reshape(blocks, block_rows, local_heads, head_dim)

        def attend_back(carry, item):
            key_sum, value_sum = carry
            q_blk, allow_blk, lse_blk, dh_blk = item
            scores = (
                jnp.einsum("qhd,khd->hqk", q_blk, keys, preferred_element_type=jnp.float32) * scale
            )
            scores = jnp.where(allow_blk[None], scores, NEG)
            prob = jnp.exp(scores - lse_blk[:, :, None])
            prob_low = prob.astype(jnp.bfloat16)
            d_prob = jnp.einsum("qhd,khd->hqk", dh_blk, values, preferred_element_type=jnp.float32)
            d_scores = (prob * (d_prob - jnp.sum(prob * d_prob, axis=2, keepdims=True))).astype(
                jnp.bfloat16
            )
            d_query = (
                jnp.einsum("hqk,khd->qhd", d_scores, keys, preferred_element_type=jnp.float32)
                * scale
            ).astype(jnp.bfloat16)
            key_sum = (
                key_sum
                + jnp.einsum("hqk,qhd->khd", d_scores, q_blk, preferred_element_type=jnp.float32)
                * scale
            )
            value_sum = value_sum + jnp.einsum(
                "hqk,qhd->khd", prob_low, dh_blk, preferred_element_type=jnp.float32
            )
            return ((key_sum, value_sum), d_query)

        zero_kv = jnp.zeros((seq_len, local_heads, head_dim), jnp.float32)
        (key_sum, value_sum), d_query = lax.scan(
            attend_back, (zero_kv, zero_kv), (q_blocks, a_blocks, logsum, dh_blocks)
        )
        d_keys, d_values = (
            lax.psum_scatter(
                key_sum.reshape(seq_len, local_width), "ctx", scatter_dimension=0, tiled=True
            ),
            lax.psum_scatter(
                value_sum.reshape(seq_len, local_width), "ctx", scatter_dimension=0, tiled=True
            ),
        )
        d_qkv = jnp.stack(
            [
                d_query.reshape(tokens, local_width),
                d_keys.astype(jnp.bfloat16),
                d_values.astype(jnp.bfloat16),
            ]
        )
        grad_qkv = jnp.einsum("td,kte->kde", h1, d_qkv, preferred_element_type=jnp.float32)
        n1_back = jnp.einsum("kte,kde->td", d_qkv, qkv_full, preferred_element_type=jnp.float32)
        first_norm_gradient = lax.psum(n1_back, "tp")
        input_gradient_list.append(
            middle_gradient
            + norm_backward(
                first_norm_gradient, normalized_first1, inverse_deviation1, norm_gains[0]
            )
        )
        acc_gains = acc_gains + jnp.stack(
            [
                jnp.sum(first_norm_gradient * normalized_first1, axis=0),
                jnp.sum(second_norm_gradient * normalized_second2, axis=0),
            ]
        )
        acc_shifts = acc_shifts + jnp.stack(
            [jnp.sum(first_norm_gradient, axis=0), jnp.sum(second_norm_gradient, axis=0)]
        )
        acc_qkv = acc_qkv + grad_qkv
        acc_out = acc_out + grad_out
        acc_up = acc_up + grad_up
        acc_down = acc_down + grad_down
    whole_qkv, whole_out, whole_up, whole_down, whole_gains, whole_shifts = lax.psum(
        (acc_qkv, acc_out, acc_up, acc_down, acc_gains, acc_shifts), "ctx"
    )
    owned = (
        lax.psum_scatter(whole_qkv, "dp", scatter_dimension=1, tiled=True),
        lax.psum_scatter(whole_out, "dp", scatter_dimension=1, tiled=True),
        lax.psum_scatter(whole_up, "dp", scatter_dimension=0, tiled=True),
        lax.psum_scatter(whole_down, "dp", scatter_dimension=1, tiled=True),
        lax.psum_scatter(whole_gains, "dp", scatter_dimension=1, tiled=True),
        lax.psum_scatter(whole_shifts, "dp", scatter_dimension=1, tiled=True),
    )
    block_out = jnp.stack(results)[:, None]
    grad_in = jnp.stack(input_gradient_list)[:, None]
    return (block_out, grad_in, owned[0], owned[1], owned[2], owned[3], owned[4], owned[5])


def solution(mesh):
    in_specs = (
        P(None, "dp", "ctx", None),
        P(None, "dp"),
        P(),
        P(None, "dp", "tp"),
        P("tp", "dp"),
        P("dp", "tp"),
        P("tp", "dp"),
        P(None, "dp"),
        P(None, "dp"),
        P(None, "dp", "ctx", None),
    )
    out_specs = (
        P(None, "dp", "ctx", None),
        P(None, "dp", "ctx", None),
        P(None, "dp", "tp"),
        P("tp", "dp"),
        P("dp", "tp"),
        P("tp", "dp"),
        P(None, "dp"),
        P(None, "dp"),
    )
    return jax.shard_map(body, mesh=mesh, in_specs=in_specs, out_specs=out_specs, check_vma=False)
```

profile of v0, /device:TPU:0, one launch (start us, length us, event | category | flops | bytes accessed | tf_op | source)
XLA Modules:
  0.0 766.6 jit_solution(9417610063547408217)
XLA Ops:
  10.2 5.5 all_gather.20
  15.7 4.5 all_gather.21
  22.8 5.9 all_gather.49
  28.7 9.4 %all_gather.22 = bf16[3,768,192]{1,2,0:T(8,128)(2,1)S(1)} all-gather(bf16[3,384,192]{1,2,0:T(8,128)(2,1)S(1)} %copy-done.43), channel_id=1, replica_groups=mesh['dp'=2,'ctx'=4,'tp'=4] {'dp'}, dimensions={1}, use_global_device_ids=true | all-gather | bytes 1327104 | tf_op jit(solution)/shard_map/all_gather | solution.py:53
  39.8 19.5 %all-gather.3 = bf16[1,2048,192]{1,2,0:T(8,128)(2,1)S(1)} all-gather(bf16[1,512,192]{1,2,0:T(8,128)(2,1)S(1)} %get-tuple-element.187), channel_id=5, replica_groups=mesh['dp'=2,'ctx'=4,'tp'=4] {'ctx'}, dimensions={1}, use_global_device_ids=true | all-gather | bytes 983040 | tf_op jit(solution)/shard_map/all_gather | solution.py:113
  59.3 17.9 %all-gather.2 = bf16[1,2048,192]{1,2,0:T(8,128)(2,1)S(1)} all-gather(bf16[1,512,192]{1,2,0:T(8,128)(2,1)S(1)} %get-tuple-element.189), channel_id=4, replica_groups=mesh['dp'=2,'ctx'=4,'tp'=4] {'ctx'}, dimensions={1}, use_global_device_ids=true | all-gather | bytes 983040 | tf_op jit(solution)/shard_map/all_gather | solution.py:114
  78.2 17.1 %all-gather.1 = bf16[1,2048,192]{1,2,0:T(8,128)(2,1)S(1)} all-gather(bf16[1,512,192]{1,2,0:T(8,128)(2,1)S(1)} %get-tuple-element.184), channel_id=3, replica_groups=mesh['dp'=2,'ctx'=4,'tp'=4] {'ctx'}, dimensions={1}, use_global_device_ids=true | all-gather | bytes 983040 | tf_op jit(solution)/shard_map/all_gather | solution.py:113
  95.3 15.7 %all-gather = bf16[1,2048,192]{1,2,0:T(8,128)(2,1)S(1)} all-gather(bf16[1,512,192]{1,2,0:T(8,128)(2,1)S(1)} %get-tuple-element.186), channel_id=2, replica_groups=mesh['dp'=2,'ctx'=4,'tp'=4] {'ctx'}, dimensions={1}, use_global_device_ids=true | all-gather | bytes 983040 | tf_op jit(solution)/shard_map/all_gather | solution.py:114
  114.5 2.7 fusion.124
  119.1 2.6 copy-done
  121.7 3.6 fusion.65
  126.9 2.7 fusion.123
  131.5 2.6 copy-done.1
  134.1 3.1 fusion.64
  140.2 68.0 %all-reduce.14.cloned.1.call-done = (f32[512,768]{1,0:T(8,128)}, f32[512,768]{1,0:T(8,128)}) async-done(((f32[512,768]{1,0:T(8,128)}, f32[512,768]{1,0:T(8,128)}), (f32[512,768]{1,0:T(8,128)}, f32[512,768]{1,0:T(8,128)})) %all-reduce.14.cloned.1.call-update) | async-done | bytes 3145744 | tf_op jit(solution)/shard_map/psum | solution.py:137
  208.2 2.4 fusion.116
  211.8 3.9 fusion.114
  217.8 3.6 fusion.56
  227.0 68.7 %all-reduce.12.cloned.1.call-done = (f32[512,768]{1,0:T(8,128)}, f32[512,768]{1,0:T(8,128)}) async-done(((f32[512,768]{1,0:T(8,128)}, f32[512,768]{1,0:T(8,128)}), (f32[512,768]{1,0:T(8,128)}, f32[512,768]{1,0:T(8,128)})) %all-reduce.12.cloned.1.call-update) | async-done | bytes 3145744 | tf_op jit(solution)/shard_map/psum | solution.py:158
  295.7 3.8 multiply_reduce_fusion.3
  303.7 7.9 %fusion.6 = f32[3,64,2048]{2,1,0:T(8,128)} fusion(bf16[512,3,64]{0,2,1:T(8,128)(2,1)S(1)} %bitcast.237, f32[3,512,2048]{2,1,0:T(8,128)} %copy-done, f32[3,512]{1,0:T(4,128)S(1)} %log_add_fusion.1), kind=kOutput, calls=%fused_computation.17 | convolution fusion | flops 408944640 | bytes 14358528 | tf_op jit(solution)/shard_map/while/body/eval_jaxpr/hqk,qhd->khd/dot_general | solution.py:191
  313.8 8.2 %fusion.4 = f32[3,64,2048]{2,1,0:T(8,128)} fusion(bf16[512,3,64]{0,2,1:T(8,128)(2,1)S(1)} %bitcast.239, f32[3,512,2048]{2,1,0:T(8,128)} %copy-done.1, f32[3,512]{1,0:T(4,128)S(1)} %log_add_fusion), kind=kOutput, calls=%fused_computation.16 | convolution fusion | flops 408944640 | bytes 14358528 | tf_op jit(solution)/shard_map/while/body/eval_jaxpr/hqk,qhd->khd/dot_general | solution.py:191
  322.9 6.6 multiply_reduce_fusion
  329.5 6.5 multiply_convert_fusion
  336.0 2.9 convolution_multiply_fusion
  339.9 6.6 multiply_reduce_fusion.1
  346.6 6.4 multiply_convert_fusion.1
  353.0 2.9 convolution_multiply_fusion.1
  356.6 4.1 fusion.112
  360.7 3.9 fusion.111
  364.6 5.6 fusion.63
  370.2 2.7 fusion.62
  374.0 10.4 %reduce-scatter.21.cloned.1.call-done = f32[512,192]{0,1:T(8,128)} async-done(((f32[2048,192]{0,1:T(8,128)}), f32[512,192]{0,1:T(8,128)}) %reduce-scatter.21.cloned.1.call-update) | async-done | bytes 393232 | tf_op jit(solution)/shard_map/reduce_scatter | solution.py:204
  385.4 35.6 %reduce-scatter.19.cloned.1.call-done = f32[512,192]{0,1:T(8,128)} async-done(((f32[2048,192]{0,1:T(8,128)}), f32[512,192]{0,1:T(8,128)}) %reduce-scatter.19.cloned.1.call-update) | async-done | bytes 393232 | tf_op jit(solution)/shard_map/reduce_scatter | solution.py:201
  422.7 3.2 convolution_bitcast_fusion
  426.0 31.6 %reduce-scatter.15.cloned.1.call-done = f32[512,192]{0,1:T(8,128)} async-done(((f32[2048,192]{0,1:T(8,128)}), f32[512,192]{0,1:T(8,128)}) %reduce-scatter.15.cloned.1.call-update) | async-done | bytes 393232 | tf_op jit(solution)/shard_map/reduce_scatter | solution.py:201
  459.3 3.3 convolution_bitcast_fusion.1
  466.7 3.1 fusion.113
  469.8 2.5 convolution_add_fusion.1
  472.4 2.9 fusion.73
  475.3 2.6 convolution_add_fusion
  483.8 97.4 %all-reduce.10.cloned.1.call-done = (f32[512,768]{1,0:T(8,128)}, f32[512,768]{1,0:T(8,128)}, f32[512,768]{1,0:T(8,128)}, f32[512,768]{1,0:T(8,128)}) async-done(((f32[512,768]{1,0:T(8,128)}, f32[512,768]{1,0:T(8,128)}, f32[512,768]{1,0:T(8,128)}, f32[512,768]{1,0:T(8,128)}), (f32[512,768]{1,0:T(8,128)}, f32[512,768]{1,0:T(8,128)}, f32[512,768]{1,0:T(8,128)}, ...) | async-done | bytes 6291472 | tf_op jit(solution)/shard_map/psum | solution.py:146
  581.2 2.9 fusion.44
  595.7 5.8 reduce-scatter.33.cloned.1.call-done
  602.5 15.0 %reduce-scatter.31.cloned.1.call-done = f32[384,2]{1,0:T(8,128)} async-done(((f32[768,2]{1,0:T(8,128)}), f32[384,2]{1,0:T(8,128)}) %reduce-scatter.31.cloned.1.call-update) | async-done | bytes 3088
  618.5 12.6 %all-reduce.3 = (f32[2,384]{1,0:T(2,128)}, f32[2,384]{1,0:T(2,128)}) all-reduce(f32[2,384]{1,0:T(2,128)S(1)} %copy.25, f32[2,384]{1,0:T(2,128)S(1)} %copy.27), channel_id=1, replica_groups=mesh['dp'=2,'ctx'=4,'tp'=4] {'ctx'}, use_global_device_ids=true, to_apply=%region_48.49 | all-reduce | flops 1536 | bytes 12288 | tf_op jit(solution)/shard_map/psum | solution.py:237
  631.1 122.6 %all-reduce.16.cloned.1.call-done = (f32[3,384,192]{1,2,0:T(8,128)}, f32[192,384]{1,0:T(8,128)}, f32[384,768]{1,0:T(8,128)}, f32[768,384]{1,0:T(8,128)}) async-done(((f32[3,384,192]{1,2,0:T(8,128)}, f32[192,384]{1,0:T(8,128)}, f32[384,768]{1,0:T(8,128)}, f32[768,384]{1,0:T(8,128)}), (f32[3,384,192]{1,2,0:T(8,128)}, f32[192,384]{1,0:T(8,128)}, f32[384,768]{1,0:T(8,128)}, ...) | async-done | bytes 3538960 | tf_op jit(solution)/shard_map/psum | solution.py:237
  753.8 2.2 copy.40
  (289 shorter events, 68.2 us)
Async XLA Ops:
  8.0 14.0 %copy-start.4 = (bf16[2,1,512,768]{3,2,1,0:T(8,128)(2,1)S(1)}, bf16[2,1,512,768]{3,2,1,0:T(8,128)(2,1)}, u32[]{:S(2)}) copy-start(bf16[2,1,512,768]{3,2,1,0:T(8,128)(2,1)} %param.10) | copy-start | bytes 4718596
  8.0 200.2 %all-reduce.14.cloned.1.call-start = ((), (), s32[]{:S(2)}) async-start(), calls=%async_computation.24 | async-start | bytes 6291456 | tf_op jit(solution)/shard_map/psum | solution.py:137
  20.2 56.9 %copy-start.73 = (f32[768]{0:T(1024)}, f32[768]{0:T(1024)S(1)}, u32[]{:S(2)}) copy-start(f32[768]{0:T(1024)S(1)} %get-tuple-element.159) | copy-start | bytes 9220
  20.3 195.5 %copy-start.67 = (f32[768]{0:T(1024)}, f32[768]{0:T(1024)S(1)}, u32[]{:S(2)}) copy-start(f32[768]{0:T(1024)S(1)} %get-tuple-element.158) | copy-start | bytes 9220
  20.3 8.4 %copy-start.43 = (bf16[3,384,192]{1,2,0:T(8,128)(2,1)S(1)}, bf16[3,384,192]{1,2,0:T(8,128)(2,1)}, u32[]{:S(2)}) copy-start(bf16[3,384,192]{1,2,0:T(8,128)(2,1)} %param.13) | copy-start | bytes 1327108
  22.0 16.1 %copy-start.54 = (f32[512]{0:T(512)}, f32[512]{0:T(512)S(1)}, u32[]{:S(2)}) copy-start(f32[512]{0:T(512)S(1)} %broadcast_multiply_fusion.9) | copy-start | bytes 6148
  22.7 54.5 %copy-start.60 = (f32[512]{0:T(512)}, f32[512]{0:T(512)S(1)}, u32[]{:S(2)}) copy-start(f32[512]{0:T(512)S(1)} %add_rsqrt_fusion.3) | copy-start | bytes 6148
  22.7 16.3 %copy-start.62 = (f32[512]{0:T(512)}, f32[512]{0:T(512)S(1)}, u32[]{:S(2)}) copy-start(f32[512]{0:T(512)S(1)} %add_rsqrt_fusion.1) | copy-start | bytes 6148
  38.1 39.1 %copy-start.32 = (bf16[3,768,192]{1,2,0:T(8,128)(2,1)}, bf16[3,768,192]{1,2,0:T(8,128)(2,1)S(1)}, u32[]{:S(2)}) copy-start(bf16[3,768,192]{1,2,0:T(8,128)(2,1)S(1)} %all_gather.22) | copy-start | bytes 2654212
  59.3 67.6 %copy-start.17 = (bf16[1,2048,192]{1,2,0:T(8,128)(2,1)}, bf16[1,2048,192]{1,2,0:T(8,128)(2,1)S(1)}, u32[]{:S(2)}) copy-start(bf16[1,2048,192]{1,2,0:T(8,128)(2,1)S(1)} %all-gather.3) | copy-start | bytes 2359300
  77.2 54.3 %copy-start.16 = (bf16[1,2048,192]{1,2,0:T(8,128)(2,1)}, bf16[1,2048,192]{1,2,0:T(8,128)(2,1)S(1)}, u32[]{:S(2)}) copy-start(bf16[1,2048,192]{1,2,0:T(8,128)(2,1)S(1)} %all-gather.2) | copy-start | bytes 2359300
  78.2 36.3 %copy-start.39 = (bf16[1,512,192]{1,2,0:T(8,128)(2,1)}, bf16[1,512,192]{1,2,0:T(8,128)(2,1)S(1)}, u32[]{:S(2)}) copy-start(bf16[1,512,192]{1,2,0:T(8,128)(2,1)S(1)} %get-tuple-element.185) | copy-start | bytes 589828
  95.3 21.9 %copy-start.19 = (bf16[1,2048,192]{1,2,0:T(8,128)(2,1)}, bf16[1,2048,192]{1,2,0:T(8,128)(2,1)S(1)}, u32[]{:S(2)}) copy-start(bf16[1,2048,192]{1,2,0:T(8,128)(2,1)S(1)} %all-gather.1) | copy-start | bytes 2359300
  111.0 8.1 %copy-start.15 = (bf16[1,2048,192]{1,2,0:T(8,128)(2,1)}, bf16[1,2048,192]{1,2,0:T(8,128)(2,1)S(1)}, u32[]{:S(2)}) copy-start(bf16[1,2048,192]{1,2,0:T(8,128)(2,1)S(1)} %all-gather) | copy-start | bytes 2359300
  117.2 4.5 copy-start
  125.3 4.3 copy-start.35
  129.6 4.5 copy-start.1
  138.8 73.0 %all-gather.7.cloned.1.call-start = ((), (), s32[]{:S(2)}) async-start(), calls=%async_computation.10 | async-start | bytes 1769472 | tf_op jit(solution)/shard_map/all_gather | solution.py:55
  139.3 78.5 %all-gather.9.cloned.1.call-start = ((), (), s32[]{:S(2)}) async-start(), calls=%async_computation.11 | async-start | bytes 1769472 | tf_op jit(solution)/shard_map/all_gather | solution.py:56
  139.9 155.8 %all-reduce.12.cloned.1.call-start = ((), (), s32[]{:S(2)}) async-start(), calls=%async_computation.23 | async-start | bytes 6291456 | tf_op jit(solution)/shard_map/psum | solution.py:158
  210.6 88.9 %copy-start.56 = (f32[512]{0:T(512)}, f32[512]{0:T(512)S(1)}, u32[]{:S(2)}) copy-start(f32[512]{0:T(512)S(1)} %broadcast_multiply_fusion.10) | copy-start | bytes 6148
  211.8 87.8 %copy-start.58 = (f32[512]{0:T(512)}, f32[512]{0:T(512)S(1)}, u32[]{:S(2)}) copy-start(f32[512]{0:T(512)S(1)} %add_rsqrt_fusion) | copy-start | bytes 6148
  211.8 87.8 %copy-start.65 = (f32[512]{0:T(512)}, f32[512]{0:T(512)S(1)}, u32[]{:S(2)}) copy-start(f32[512]{0:T(512)S(1)} %add_rsqrt_fusion.2) | copy-start | bytes 6148
  211.8 3.9 copy-start.78
  226.9 146.0 %reduce-scatter.17.cloned.1.call-start = ((), (), s32[]{:S(2)}) async-start(), calls=%async_computation.13 | async-start | bytes 1966080 | tf_op jit(solution)/shard_map/reduce_scatter | solution.py:204
  295.7 4.3 copy-start.26
  303.7 7.9 %copy-start.21 = (bf16[512,192]{0,1:T(8,128)(2,1)}, bf16[512,192]{0,1:T(8,128)(2,1)S(1)}, u32[]{:S(2)}) copy-start(bf16[512,192]{0,1:T(8,128)(2,1)S(1)} %convolution_convert_fusion.1) | copy-start | bytes 589828
  311.6 72.8 %reduce-scatter.21.cloned.1.call-start = ((), (), s32[]{:S(2)}) async-start(), calls=%async_computation.15 | async-start | bytes 1966080 | tf_op jit(solution)/shard_map/reduce_scatter | solution.py:204
  313.8 8.2 %copy-start.23 = (bf16[512,192]{0,1:T(8,128)(2,1)}, bf16[512,192]{0,1:T(8,128)(2,1)S(1)}, u32[]{:S(2)}) copy-start(bf16[512,192]{0,1:T(8,128)(2,1)S(1)} %convolution_convert_fusion) | copy-start | bytes 589828
  322.0 99.0 %reduce-scatter.19.cloned.1.call-start = ((), (), s32[]{:S(2)}) async-start(), calls=%async_computation.14 | async-start | bytes 1966080 | tf_op jit(solution)/shard_map/reduce_scatter | solution.py:201
  329.5 6.5 copy-start.42
  339.0 118.6 %reduce-scatter.15.cloned.1.call-start = ((), (), s32[]{:S(2)}) async-start(), calls=%async_computation.12 | async-start | bytes 1966080 | tf_op jit(solution)/shard_map/reduce_scatter | solution.py:201
  346.5 6.5 copy-start.40
  356.3 224.9 %all-reduce.10.cloned.1.call-start = ((), (), s32[]{:S(2)}) async-start(), calls=%async_computation.22 | async-start | bytes 12582912 | tf_op jit(solution)/shard_map/psum | solution.py:146
  356.6 4.1 copy-start.77
  356.6 13.6 %slice-start = ((s8[6291456]{0:T(1024)(128)(4,1)}), s8[4194304]{0:T(1024)(128)(4,1)S(1)}, s32[]{:S(2)}) async-start(s8[6291456]{0:T(1024)(128)(4,1)} %bitcast.223), calls=%async_computation.26 | async-start | bytes 8388608
  360.7 9.5 %slice-start.1 = ((s8[6291456]{0:T(1024)(128)(4,1)}), s8[2097152]{0:T(1024)(128)(4,1)S(1)}, s32[]{:S(2)}) async-start(s8[6291456]{0:T(1024)(128)(4,1)} %bitcast.223), calls=%async_computation.27 | async-start | bytes 4194304
  364.6 5.6 copy-start.20
  374.0 84.7 %copy-start.45 = (bf16[1,512,192]{1,2,0:T(8,128)(2,1)}, bf16[1,512,192]{1,2,0:T(8,128)(2,1)S(1)}, u32[]{:S(2)}) copy-start(bf16[1,512,192]{1,2,0:T(8,128)(2,1)S(1)} %convert_bitcast_fusion.6) | copy-start | bytes 589828
  385.4 40.5 %copy-start.47 = (bf16[1,512,192]{1,2,0:T(8,128)(2,1)}, bf16[1,512,192]{1,2,0:T(8,128)(2,1)S(1)}, u32[]{:S(2)}) copy-start(bf16[1,512,192]{1,2,0:T(8,128)(2,1)S(1)} %convert_bitcast_fusion.4) | copy-start | bytes 589828
  462.6 123.6 %reduce-scatter.25.cloned.1.call-start = ((), (), s32[]{:S(2)}) async-start(), calls=%async_computation.17 | async-start | bytes 884736 | tf_op jit(solution)/shard_map/reduce_scatter | solution.py:242
  466.6 119.7 %reduce-scatter.27.cloned.1.call-start = ((), (), s32[]{:S(2)}) async-start(), calls=%async_computation.18 | async-start | bytes 3538944 | tf_op jit(solution)/shard_map/reduce_scatter | solution.py:243
  472.3 114.0 %reduce-scatter.29.cloned.1.call-start = ((), (), s32[]{:S(2)}) async-start(), calls=%async_computation.19 | async-start | bytes 3538944 | tf_op jit(solution)/shard_map/reduce_scatter | solution.py:244
  478.0 108.3 %reduce-scatter.23.cloned.1.call-start = ((), (), s32[]{:S(2)}) async-start(), calls=%async_computation.16 | async-start | bytes 2654208 | tf_op jit(solution)/shard_map/reduce_scatter | solution.py:241
  483.1 98.1 %copy-start.64 = (f32[512]{0:T(512)S(1)}, f32[512]{0:T(512)}, u32[]{:S(2)}) copy-start(f32[512]{0:T(512)} %copy-done.62) | copy-start | bytes 6148
  483.1 118.4 %reduce-scatter.33.cloned.1.call-start = ((), (), s32[]{:S(2)}) async-start(), calls=%async_computation.21 | async-start | bytes 589824
  585.1 32.4 %reduce-scatter.31.cloned.1.call-start = ((), (), s32[]{:S(2)}) async-start(), calls=%async_computation.20 | async-start | bytes 589824
  586.2 167.6 %all-reduce.16.cloned.1.call-start = ((), (), s32[]{:S(2)}) async-start(), calls=%async_computation.25 | async-start | bytes 7077888 | tf_op jit(solution)/shard_map/psum | solution.py:237
  (53 other events, 114.5 us)
Sparse Core Ops, SparseCore 0:
  138.9 69.2 all-reduce.13
  227.1 68.5 all-reduce.11
  462.7 118.4 all-reduce.9
Sparse Core Ops, SparseCore 1:
  140.8 23.4 all-gather.6
  165.7 22.6 all-gather.8
  311.7 35.5 reduce-scatter.16
  350.2 34.2 reduce-scatter.20
  386.7 34.2 reduce-scatter.18
  423.4 34.2 reduce-scatter.14
  466.7 14.0 reduce-scatter.24
  483.5 34.7 reduce-scatter.26
  520.3 34.7 reduce-scatter.28
  557.4 28.2 reduce-scatter.22
  588.3 13.1 reduce-scatter.32
  604.3 13.1 reduce-scatter.30
  620.0 133.7 all-reduce.15
where the time goes:
time: 775 us; the launch traced here: 767 us
  waiting for transfers between devices  457 us (59%)
  matrix products  110 us (14%)
  blocking collectives  108 us (14%)
  other arithmetic  46.1 us (6%)
  local copies, waits for them, and re-layouts  26.5 us (3%)
  between operations  17.2 us (2%)
    psum x1, waiting for transfers between devices, body(): lax.psum((acc_qkv, acc_out, acc_up, acc_down, acc_gains, acc_shifts), 'ctx')  123 us
    psum x1, waiting for transfers between devices, body(): mlp = lax.psum(mlp_part, 'tp')  97.4 us
    psum x1, waiting for transfers between devices, body(): second_norm_gradient = lax.psum(n2_back, 'tp')  68.7 us
    psum x1, waiting for transfers between devices, body(): attn = lax.psum(attn_part, 'tp')  68 us
    reduce_scatter x2, waiting for transfers between devices, body(): lax.psum_scatter(key_sum.reshape(seq_len, local_width), 'ctx', scatter_di...  67.2 us
    all_gather x2, blocking collectives, body(): lax.all_gather(qkv[1], 'ctx', axis=0, tiled=True)  36.6 us
    all_gather x2, blocking collectives, body(): lax.all_gather(qkv[2], 'ctx', axis=0, tiled=True)  33.6 us
    unnamed x178, local copies, waits for them, and re-layouts  24.3 us
  transfers between devices with their start and end apart: 16, of which 9 were waited for; matrix products, arithmetic and copies ran while one was open for 14% of the time, Pallas kernels for 0%

commit v1 on v0

--- a/solution.py
+++ b/solution.py
@@ -143,7 +143,9 @@
         up = jnp.dot(h2, up_full, preferred_element_type=jnp.float32)
         act = gelu_value(up).astype(jnp.bfloat16)
         mlp_part = jnp.dot(act, down_full, preferred_element_type=jnp.float32)
-        mlp = lax.psum(mlp_part, "tp")
+        mlp = mlp_part
+        for hop in (1, 2):
+            mlp = mlp + lax.ppermute(mlp, "tp", [(dev, dev ^ hop) for dev in range(4)])
         results.append((middle_state + branch * mlp).astype(jnp.bfloat16))
         qkv_full, out_full, up_full, down_full, gains_full, shifts_full = fetch_weights(
             qkv_weight, out_weight, up_weight, down_weight, ln_gains, ln_shifts

time: 775 us -> 830 us (1.071)
  waiting for transfers between devices: 457 us -> 510 us
  other arithmetic: 46.1 us -> 57.3 us
  matrix products: 110 us -> 99.3 us
    psum x1, waiting for transfers between devices: 97.4 us -> 46.9 us  [body(): first_norm_gradient = lax.psum(n1_back, 'tp')]
    psum x1, waiting for transfers between devices: 68.7 us -> 111 us  [body(): second_norm_gradient = lax.psum(n2_back, 'tp')]
    reduce_scatter x1, waiting for transfers between devices: 0.02 us -> 30.6 us  [body(): lax.psum_scatter(whole_qkv, 'dp', scatter_dimension=1, tiled=True)]
    reduce_scatter x1, waiting for transfers between devices: 0.02 us -> 20 us  [body(): lax.psum_scatter(whole_up, 'dp', scatter_dimension=0, tiled=True)]
    reduce_scatter x2, waiting for transfers between devices: 10.4 us -> 18.8 us  [body(): lax.psum_scatter(value_sum.reshape(seq_len, local_width), 'ctx', scatter_...]
    unnamed x178 -> x170, local copies, waits for them, and re-layouts: 24.3 us -> 24.5 us
  transfers between devices with their start and end apart: 16 -> 20, of which waited for: 9 -> 12; matrix products, arithmetic and copies ran while one was open for 14% -> 14% of each run, Pallas kernels for 0% -> 0%
where the time goes in v1:
time: 830 us; the launch traced here: 822 us
  waiting for transfers between devices  510 us (61%)
  blocking collectives  108 us (13%)
  matrix products  99.3 us (12%)
  other arithmetic  57.3 us (7%)
  local copies, waits for them, and re-layouts  26.7 us (3%)
  between operations  17.2 us (2%)
    psum x1, waiting for transfers between devices, body(): lax.psum((acc_qkv, acc_out, acc_up, acc_down, acc_gains, acc_shifts), 'ctx')  123 us
    psum x1, waiting for transfers between devices, body(): second_norm_gradient = lax.psum(n2_back, 'tp')  111 us
    psum x1, waiting for transfers between devices, body(): attn = lax.psum(attn_part, 'tp')  68 us
    reduce_scatter x2, waiting for transfers between devices, body(): lax.psum_scatter(key_sum.reshape(seq_len, local_width), 'ctx', scatter_di...  67.1 us
    psum x1, waiting for transfers between devices, body(): first_norm_gradient = lax.psum(n1_back, 'tp')  46.9 us
    all_gather x2, blocking collectives, body(): lax.all_gather(qkv[1], 'ctx', axis=0, tiled=True)  36.6 us
    all_gather x2, blocking collectives, body(): lax.all_gather(qkv[2], 'ctx', axis=0, tiled=True)  33.6 us
    reduce_scatter x1, waiting for transfers between devices, body(): lax.psum_scatter(whole_qkv, 'dp', scatter_dimension=1, tiled=True)  30.6 us
  transfers between devices with their start and end apart: 20, of which 12 were waited for; matrix products, arithmetic and copies ran while one was open for 14% of the time, Pallas kernels for 0%

profile of v1, /device:TPU:0, one launch (start us, length us, event | category | flops | bytes accessed | tf_op | source)
XLA Modules:
  0.0 821.7 jit_solution(5533331327220144784)
XLA Ops:
  10.2 5.5 all_gather.20
  15.7 4.5 all_gather.21
  22.8 5.9 all_gather.49
  28.8 9.4 %all_gather.22 = bf16[3,768,192]{1,2,0:T(8,128)(2,1)S(1)} all-gather(bf16[3,384,192]{1,2,0:T(8,128)(2,1)S(1)} %copy-done.38), channel_id=1, replica_groups=mesh['dp'=2,'ctx'=4,'tp'=4] {'dp'}, dimensions={1}, use_global_device_ids=true | all-gather | bytes 1327104 | tf_op jit(solution)/shard_map/all_gather | solution.py:53
  39.8 19.5 %all-gather.3 = bf16[1,2048,192]{1,2,0:T(8,128)(2,1)S(1)} all-gather(bf16[1,512,192]{1,2,0:T(8,128)(2,1)S(1)} %get-tuple-element.187), channel_id=5, replica_groups=mesh['dp'=2,'ctx'=4,'tp'=4] {'ctx'}, dimensions={1}, use_global_device_ids=true | all-gather | bytes 983040 | tf_op jit(solution)/shard_map/all_gather | solution.py:113
  59.3 17.8 %all-gather.2 = bf16[1,2048,192]{1,2,0:T(8,128)(2,1)S(1)} all-gather(bf16[1,512,192]{1,2,0:T(8,128)(2,1)S(1)} %get-tuple-element.189), channel_id=4, replica_groups=mesh['dp'=2,'ctx'=4,'tp'=4] {'ctx'}, dimensions={1}, use_global_device_ids=true | all-gather | bytes 983040 | tf_op jit(solution)/shard_map/all_gather | solution.py:114
  78.2 17.1 %all-gather.1 = bf16[1,2048,192]{1,2,0:T(8,128)(2,1)S(1)} all-gather(bf16[1,512,192]{1,2,0:T(8,128)(2,1)S(1)} %get-tuple-element.184), channel_id=3, replica_groups=mesh['dp'=2,'ctx'=4,'tp'=4] {'ctx'}, dimensions={1}, use_global_device_ids=true | all-gather | bytes 983040 | tf_op jit(solution)/shard_map/all_gather | solution.py:113
  95.3 15.7 %all-gather = bf16[1,2048,192]{1,2,0:T(8,128)(2,1)S(1)} all-gather(bf16[1,512,192]{1,2,0:T(8,128)(2,1)S(1)} %get-tuple-element.186), channel_id=2, replica_groups=mesh['dp'=2,'ctx'=4,'tp'=4] {'ctx'}, dimensions={1}, use_global_device_ids=true | all-gather | bytes 983040 | tf_op jit(solution)/shard_map/all_gather | solution.py:114
  114.5 2.7 fusion.124
  119.1 2.6 copy-done
  121.7 3.6 fusion.65
  126.9 2.7 fusion.123
  134.1 3.1 fusion.64
  140.8 68.0 %all-reduce.14.cloned.1.call-done = (f32[512,768]{1,0:T(8,128)}, f32[512,768]{1,0:T(8,128)}) async-done(((f32[512,768]{1,0:T(8,128)}, f32[512,768]{1,0:T(8,128)}), (f32[512,768]{1,0:T(8,128)}, f32[512,768]{1,0:T(8,128)})) %all-reduce.14.cloned.1.call-update) | async-done | bytes 3145744 | tf_op jit(solution)/shard_map/psum | solution.py:137
  212.4 3.8 fusion.114
  216.2 4.1 fusion.111
  231.8 3.3 add.315
  235.5 3.5 add.325
  240.4 110.8 %all-reduce.12.cloned.1.call-done = (f32[512,768]{1,0:T(8,128)}, f32[512,768]{1,0:T(8,128)}) async-done(((f32[512,768]{1,0:T(8,128)}, f32[512,768]{1,0:T(8,128)}), (f32[512,768]{1,0:T(8,128)}, f32[512,768]{1,0:T(8,128)})) %all-reduce.12.cloned.1.call-update) | async-done | bytes 3145744 | tf_op jit(solution)/shard_map/psum | solution.py:160
  351.1 3.8 multiply_reduce_fusion.3
  356.2 6.2 convert_add_fusion.1
  364.5 3.3 fusion.6
  369.8 8.1 fusion.4
  378.8 6.6 multiply_reduce_fusion
  385.4 6.5 multiply_convert_fusion
  391.9 2.8 convolution_multiply_fusion
  395.9 6.6 multiply_reduce_fusion.1
  402.5 6.4 multiply_convert_fusion.1
  408.9 3.0 convolution_multiply_fusion.1
  412.2 5.9 fusion.63
  418.1 2.7 fusion.62
  421.9 18.8 %reduce-scatter.21.cloned.1.call-done = f32[512,192]{0,1:T(8,128)} async-done(((f32[2048,192]{0,1:T(8,128)}), f32[512,192]{0,1:T(8,128)}) %reduce-scatter.21.cloned.1.call-update) | async-done | bytes 393232 | tf_op jit(solution)/shard_map/reduce_scatter | solution.py:206
  441.7 35.6 %reduce-scatter.19.cloned.1.call-done = f32[512,192]{0,1:T(8,128)} async-done(((f32[2048,192]{0,1:T(8,128)}), f32[512,192]{0,1:T(8,128)}) %reduce-scatter.19.cloned.1.call-update) | async-done | bytes 393232 | tf_op jit(solution)/shard_map/reduce_scatter | solution.py:203
  479.0 3.3 convolution_bitcast_fusion
  482.2 31.6 %reduce-scatter.15.cloned.1.call-done = f32[512,192]{0,1:T(8,128)} async-done(((f32[2048,192]{0,1:T(8,128)}), f32[512,192]{0,1:T(8,128)}) %reduce-scatter.15.cloned.1.call-update) | async-done | bytes 393232 | tf_op jit(solution)/shard_map/reduce_scatter | solution.py:203
  515.5 3.4 convolution_bitcast_fusion.1
  522.9 3.1 fusion.73
  526.0 2.6 convolution_add_fusion
  529.4 2.7 fusion.113
  539.4 46.9 %all-reduce.10.cloned.1.call-done = (f32[512,768]{1,0:T(8,128)}, f32[512,768]{1,0:T(8,128)}) async-done(((f32[512,768]{1,0:T(8,128)}, f32[512,768]{1,0:T(8,128)}), (f32[512,768]{1,0:T(8,128)}, f32[512,768]{1,0:T(8,128)})) %all-reduce.10.cloned.1.call-update) | async-done | bytes 3145744 | tf_op jit(solution)/shard_map/psum | solution.py:219
  586.3 2.9 fusion.44
  591.4 20.0 %reduce-scatter.27.cloned.1.call-done = f32[384,768]{1,0:T(8,128)} async-done(((f32[768,768]{1,0:T(8,128)}), f32[384,768]{1,0:T(8,128)}) %reduce-scatter.27.cloned.1.call-update) | async-done | bytes 1179664 | tf_op jit(solution)/shard_map/reduce_scatter | solution.py:245
  611.4 30.6 %reduce-scatter.23.cloned.1.call-done = f32[3,384,192]{1,2,0:T(8,128)} async-done(((f32[3,768,192]{1,2,0:T(8,128)}), f32[3,384,192]{1,2,0:T(8,128)}) %reduce-scatter.23.cloned.1.call-update) | async-done | bytes 884752 | tf_op jit(solution)/shard_map/reduce_scatter | solution.py:243
  642.0 2.8 maximum_bitcast_fusion.1
  649.4 7.8 reduce-scatter.33.cloned.1.call-done
  658.2 14.4 %reduce-scatter.31.cloned.1.call-done = f32[384,2]{1,0:T(8,128)} async-done(((f32[768,2]{1,0:T(8,128)}), f32[384,2]{1,0:T(8,128)}) %reduce-scatter.31.cloned.1.call-update) | async-done | bytes 3088
  673.7 12.6 %all-reduce.3 = (f32[2,384]{1,0:T(2,128)}, f32[2,384]{1,0:T(2,128)}) all-reduce(f32[2,384]{1,0:T(2,128)S(1)} %copy.25, f32[2,384]{1,0:T(2,128)S(1)} %copy.27), channel_id=1, replica_groups=mesh['dp'=2,'ctx'=4,'tp'=4] {'ctx'}, use_global_device_ids=true, to_apply=%region_46.47 | all-reduce | flops 1536 | bytes 12288 | tf_op jit(solution)/shard_map/psum | solution.py:239
  686.3 122.6 %all-reduce.16.cloned.1.call-done = (f32[3,384,192]{1,2,0:T(8,128)}, f32[192,384]{1,0:T(8,128)}, f32[384,768]{1,0:T(8,128)}, f32[768,384]{1,0:T(8,128)}) async-done(((f32[3,384,192]{1,2,0:T(8,128)}, f32[192,384]{1,0:T(8,128)}, f32[384,768]{1,0:T(8,128)}, f32[768,384]{1,0:T(8,128)}), (f32[3,384,192]{1,2,0:T(8,128)}, f32[192,384]{1,0:T(8,128)}, f32[384,768]{1,0:T(8,128)}, ...) | async-done | bytes 3538960 | tf_op jit(solution)/shard_map/psum | solution.py:239
  (288 shorter events, 77.7 us)
Async XLA Ops:
  8.0 14.1 %copy-start.5 = (bf16[2,1,512,768]{3,2,1,0:T(8,128)(2,1)S(1)}, bf16[2,1,512,768]{3,2,1,0:T(8,128)(2,1)}, u32[]{:S(2)}) copy-start(bf16[2,1,512,768]{3,2,1,0:T(8,128)(2,1)} %param.10) | copy-start | bytes 4718596
  8.0 200.9 %all-reduce.14.cloned.1.call-start = ((), (), s32[]{:S(2)}) async-start(), calls=%async_computation.24 | async-start | bytes 6291456 | tf_op jit(solution)/shard_map/psum | solution.py:137
  15.7 61.5 %copy-start.51 = (f32[768]{0:T(1024)}, f32[768]{0:T(1024)S(1)}, u32[]{:S(2)}) copy-start(f32[768]{0:T(1024)S(1)} %get-tuple-element.157) | copy-start | bytes 9220
  20.3 56.9 %copy-start.69 = (f32[768]{0:T(1024)}, f32[768]{0:T(1024)S(1)}, u32[]{:S(2)}) copy-start(f32[768]{0:T(1024)S(1)} %get-tuple-element.159) | copy-start | bytes 9220
  20.3 200.1 %copy-start.63 = (f32[768]{0:T(1024)}, f32[768]{0:T(1024)S(1)}, u32[]{:S(2)}) copy-start(f32[768]{0:T(1024)S(1)} %get-tuple-element.158) | copy-start | bytes 9220
  20.3 8.5 %copy-start.38 = (bf16[3,384,192]{1,2,0:T(8,128)(2,1)S(1)}, bf16[3,384,192]{1,2,0:T(8,128)(2,1)}, u32[]{:S(2)}) copy-start(bf16[3,384,192]{1,2,0:T(8,128)(2,1)} %param.13) | copy-start | bytes 1327108
  22.0 55.1 %copy-start.53 = (f32[512]{0:T(512)}, f32[512]{0:T(512)S(1)}, u32[]{:S(2)}) copy-start(f32[512]{0:T(512)S(1)} %broadcast_multiply_fusion.11) | copy-start | bytes 6148
  22.1 16.1 %copy-start.55 = (f32[512]{0:T(512)}, f32[512]{0:T(512)S(1)}, u32[]{:S(2)}) copy-start(f32[512]{0:T(512)S(1)} %broadcast_multiply_fusion.9) | copy-start | bytes 6148
  22.7 54.5 %copy-start.57 = (f32[512]{0:T(512)}, f32[512]{0:T(512)S(1)}, u32[]{:S(2)}) copy-start(f32[512]{0:T(512)S(1)} %add_rsqrt_fusion.3) | copy-start | bytes 6148
  22.7 16.3 %copy-start.59 = (f32[512]{0:T(512)}, f32[512]{0:T(512)S(1)}, u32[]{:S(2)}) copy-start(f32[512]{0:T(512)S(1)} %add_rsqrt_fusion.1) | copy-start | bytes 6148
  38.1 39.1 %copy-start.27 = (bf16[3,768,192]{1,2,0:T(8,128)(2,1)}, bf16[3,768,192]{1,2,0:T(8,128)(2,1)S(1)}, u32[]{:S(2)}) copy-start(bf16[3,768,192]{1,2,0:T(8,128)(2,1)S(1)} %all_gather.22) | copy-start | bytes 2654212
  59.3 67.6 %copy-start.15 = (bf16[1,2048,192]{1,2,0:T(8,128)(2,1)}, bf16[1,2048,192]{1,2,0:T(8,128)(2,1)S(1)}, u32[]{:S(2)}) copy-start(bf16[1,2048,192]{1,2,0:T(8,128)(2,1)S(1)} %all-gather.3) | copy-start | bytes 2359300
  77.2 54.3 %copy-start.14 = (bf16[1,2048,192]{1,2,0:T(8,128)(2,1)}, bf16[1,2048,192]{1,2,0:T(8,128)(2,1)S(1)}, u32[]{:S(2)}) copy-start(bf16[1,2048,192]{1,2,0:T(8,128)(2,1)S(1)} %all-gather.2) | copy-start | bytes 2359300
  78.2 36.3 %copy-start.34 = (bf16[1,512,192]{1,2,0:T(8,128)(2,1)}, bf16[1,512,192]{1,2,0:T(8,128)(2,1)S(1)}, u32[]{:S(2)}) copy-start(bf16[1,512,192]{1,2,0:T(8,128)(2,1)S(1)} %get-tuple-element.185) | copy-start | bytes 589828
  95.3 21.9 %copy-start.16 = (bf16[1,2048,192]{1,2,0:T(8,128)(2,1)}, bf16[1,2048,192]{1,2,0:T(8,128)(2,1)S(1)}, u32[]{:S(2)}) copy-start(bf16[1,2048,192]{1,2,0:T(8,128)(2,1)S(1)} %all-gather.1) | copy-start | bytes 2359300
  111.0 8.1 copy-start.13
  117.2 4.5 copy-start
  139.4 73.0 %all-gather.7.cloned.1.call-start = ((), (), s32[]{:S(2)}) async-start(), calls=%async_computation.10 | async-start | bytes 1769472 | tf_op jit(solution)/shard_map/all_gather | solution.py:55
  140.0 76.2 %all-gather.9.cloned.1.call-start = ((), (), s32[]{:S(2)}) async-start(), calls=%async_computation.11 | async-start | bytes 1769472 | tf_op jit(solution)/shard_map/all_gather | solution.py:56
  140.6 210.5 %all-reduce.12.cloned.1.call-start = ((), (), s32[]{:S(2)}) async-start(), calls=%async_computation.23 | async-start | bytes 6291456 | tf_op jit(solution)/shard_map/psum | solution.py:160
  212.4 143.8 %copy-start.61 = (f32[512]{0:T(512)}, f32[512]{0:T(512)S(1)}, u32[]{:S(2)}) copy-start(f32[512]{0:T(512)S(1)} %add_rsqrt_fusion.2) | copy-start | bytes 6148
  220.3 11.5 %collective-permute-start = (f32[512,768]{1,0:T(8,128)}, f32[512,768]{1,0:T(8,128)}, u32[]{:S(2)}, u32[]{:S(2)}) collective-permute-start(f32[512,768]{1,0:T(8,128)} %fusion.111), channel_id=1, source_target_pairs={{0,1},{1,0},{2,3},{3,2},{4,5},{5,4},{6,7},{7,6},{8,9},{9,8},{10,11... | collective-permute-start | bytes 4718600 | tf_op jit(solution)/shard_map/ppermute | solution.py:148
  223.8 11.7 %collective-permute-start.2 = (f32[512,768]{1,0:T(8,128)}, f32[512,768]{1,0:T(8,128)}, u32[]{:S(2)}, u32[]{:S(2)}) collective-permute-start(f32[512,768]{1,0:T(8,128)} %fusion.112), channel_id=1, source_target_pairs={{0,1},{1,0},{2,3},{3,2},{4,5},{5,4},{6,7},{7,6},{8,9},{9,8},{10,11... | collective-permute-start | bytes 4718600 | tf_op jit(solution)/shard_map/ppermute | solution.py:148
  231.5 189.3 %reduce-scatter.17.cloned.1.call-start = ((), (), s32[]{:S(2)}) async-start(), calls=%async_computation.13 | async-start | bytes 1966080 | tf_op jit(solution)/shard_map/reduce_scatter | solution.py:206
  235.1 119.9 %collective-permute-start.1 = (f32[512,768]{1,0:T(8,128)}, f32[512,768]{1,0:T(8,128)}, u32[]{:S(2)}, u32[]{:S(2)}) collective-permute-start(f32[512,768]{1,0:T(8,128)} %add.315), channel_id=1, source_target_pairs={{0,2},{1,3},{2,0},{3,1},{4,6},{5,7},{6,4},{7,5},{8,10},{9,11},{10,... | collective-permute-start | bytes 4718600 | tf_op jit(solution)/shard_map/ppermute | solution.py:148
  239.1 117.1 %collective-permute-start.3 = (f32[512,768]{1,0:T(8,128)}, f32[512,768]{1,0:T(8,128)}, u32[]{:S(2)}, u32[]{:S(2)}) collective-permute-start(f32[512,768]{1,0:T(8,128)} %add.325), channel_id=1, source_target_pairs={{0,2},{1,3},{2,0},{3,1},{4,6},{5,7},{6,4},{7,5},{8,10},{9,11},{10,... | collective-permute-start | bytes 4718600 | tf_op jit(solution)/shard_map/ppermute | solution.py:148
  351.1 5.0 copy-start.11
  351.1 12.8 %slice-start = ((s8[12582912]{0:T(1024)(128)(4,1)}), s8[4194304]{0:T(1024)(128)(4,1)S(1)}, s32[]{:S(2)}) async-start(s8[12582912]{0:T(1024)(128)(4,1)} %bitcast.223), calls=%async_computation.26 | async-start | bytes 8388608
  356.2 7.8 slice-start.1
  356.2 8.4 %slice-start.2 = ((s8[12582912]{0:T(1024)(128)(4,1)}), s8[4194304]{0:T(1024)(128)(4,1)S(1)}, s32[]{:S(2)}) async-start(s8[12582912]{0:T(1024)(128)(4,1)} %bitcast.223), calls=%async_computation.28 | async-start | bytes 8388608
  367.9 72.8 %reduce-scatter.21.cloned.1.call-start = ((), (), s32[]{:S(2)}) async-start(), calls=%async_computation.15 | async-start | bytes 1966080 | tf_op jit(solution)/shard_map/reduce_scatter | solution.py:206
  369.8 8.1 copy-start.20
  377.9 99.3 %reduce-scatter.19.cloned.1.call-start = ((), (), s32[]{:S(2)}) async-start(), calls=%async_computation.14 | async-start | bytes 1966080 | tf_op jit(solution)/shard_map/reduce_scatter | solution.py:203
  385.4 6.5 copy-start.37
  395.0 118.8 %reduce-scatter.15.cloned.1.call-start = ((), (), s32[]{:S(2)}) async-start(), calls=%async_computation.12 | async-start | bytes 1966080 | tf_op jit(solution)/shard_map/reduce_scatter | solution.py:203
  402.5 6.5 copy-start.35
  412.2 174.2 %all-reduce.10.cloned.1.call-start = ((), (), s32[]{:S(2)}) async-start(), calls=%async_computation.22 | async-start | bytes 6291456 | tf_op jit(solution)/shard_map/psum | solution.py:219
  412.2 5.9 copy-start.4
  412.2 5.9 copy-start.17
  421.9 93.0 %copy-start.40 = (bf16[1,512,192]{1,2,0:T(8,128)(2,1)}, bf16[1,512,192]{1,2,0:T(8,128)(2,1)S(1)}, u32[]{:S(2)}) copy-start(bf16[1,512,192]{1,2,0:T(8,128)(2,1)S(1)} %convert_bitcast_fusion.6) | copy-start | bytes 589828
  441.7 40.5 %copy-start.42 = (bf16[1,512,192]{1,2,0:T(8,128)(2,1)}, bf16[1,512,192]{1,2,0:T(8,128)(2,1)S(1)}, u32[]{:S(2)}) copy-start(bf16[1,512,192]{1,2,0:T(8,128)(2,1)S(1)} %convert_bitcast_fusion.4) | copy-start | bytes 589828
  518.9 72.5 %reduce-scatter.25.cloned.1.call-start = ((), (), s32[]{:S(2)}) async-start(), calls=%async_computation.17 | async-start | bytes 884736 | tf_op jit(solution)/shard_map/reduce_scatter | solution.py:244
  522.9 68.6 %reduce-scatter.29.cloned.1.call-start = ((), (), s32[]{:S(2)}) async-start(), calls=%async_computation.19 | async-start | bytes 3538944 | tf_op jit(solution)/shard_map/reduce_scatter | solution.py:246
  528.7 82.7 %reduce-scatter.27.cloned.1.call-start = ((), (), s32[]{:S(2)}) async-start(), calls=%async_computation.18 | async-start | bytes 3538944 | tf_op jit(solution)/shard_map/reduce_scatter | solution.py:245
  534.7 107.3 %reduce-scatter.23.cloned.1.call-start = ((), (), s32[]{:S(2)}) async-start(), calls=%async_computation.16 | async-start | bytes 2654208 | tf_op jit(solution)/shard_map/reduce_scatter | solution.py:243
  538.7 118.5 %reduce-scatter.33.cloned.1.call-start = ((), (), s32[]{:S(2)}) async-start(), calls=%async_computation.21 | async-start | bytes 589824
  590.3 82.4 %reduce-scatter.31.cloned.1.call-start = ((), (), s32[]{:S(2)}) async-start(), calls=%async_computation.20 | async-start | bytes 589824
  591.3 217.6 %all-reduce.16.cloned.1.call-start = ((), (), s32[]{:S(2)}) async-start(), calls=%async_computation.25 | async-start | bytes 7077888 | tf_op jit(solution)/shard_map/psum | solution.py:239
  (53 other events, 105.8 us)
Sparse Core Ops, SparseCore 0:
  139.5 69.2 all-reduce.13
  231.7 119.4 all-reduce.11
  519.0 67.2 all-reduce.9
Sparse Core Ops, SparseCore 1:
  141.4 23.4 all-gather.6
  166.3 22.6 all-gather.8
  367.9 35.5 reduce-scatter.16
  406.4 34.2 reduce-scatter.20
  443.0 34.2 reduce-scatter.18
  479.6 34.2 reduce-scatter.14
  523.0 14.1 reduce-scatter.24
  539.2 34.7 reduce-scatter.28
  576.6 34.7 reduce-scatter.26
  613.7 28.2 reduce-scatter.22
  644.1 13.1 reduce-scatter.32
  659.5 13.1 reduce-scatter.30
  675.2 133.7 all-reduce.15
